TPU v7x, 256 devices: a whole 4x4x8 slice. The times are simulated.
256 devices in a mesh: band: 4 (over x_lo, core), grid: 64 (over z, y, x_hi).
Axes of the slice: x: 4 (x_hi: 2, x_lo: 2; x = x_hi * 2 + x_lo), y: 4, z: 8, core: 2. Of those that a mesh axis runs over, the one named last changes fastest.
Arguments:
- orbitals: float32 [256, 256, 8, 128], P('band', 'grid'), may hold values from -6 to 6
- potential: float32 [256, 8, 128], P('grid'), may hold values from 0 to 1.5
Outputs:
- orthonormal: float32 [256, 256, 8, 128], P('band', 'grid')
All inputs are finite; a program needn't handle non-finite values.
Results may differ from a plain program's by a relative error of at most 0.000071.
Values sent between devices are 32-bit elements; how exact they have to be, the bound alone decides.
A program may use at most 64 MiB of HBM per device.

v0:
```python
import jax
import jax.numpy as jnp
from jax import lax
from jax.sharding import PartitionSpec as P

COEFS = (-205.0 / 72.0, 8.0 / 5.0, -1.0 / 5.0, 8.0 / 315.0, -1.0 / 560.0)
CENTER = 8.0
HALF = 4.0


def with_halo(block, sides, width):
    for axis, dim in sides:
        count = lax.axis_size(axis)
        forward = [(i, i + 1) for i in range(count - 1)]
        forward.append((count - 1, 0))
        backward = [(target, source) for source, target in forward]
        low = lax.ppermute(
            lax.slice_in_dim(block, block.shape[dim] - width, None, axis=dim), axis, forward
        )
        high = lax.ppermute(lax.slice_in_dim(block, 0, width, axis=dim), axis, backward)
        block = jnp.concatenate([low, block, high], axis=dim)
    return block


def periodic_pad(field, axis):
    count = field.shape[axis]
    head = lax.slice_in_dim(field, count - 4, count, axis=axis)
    tail = lax.slice_in_dim(field, 0, 4, axis=axis)
    return jnp.concatenate([head, field, tail], axis=axis)


def add_axis(lap, padded, axis, count):
    for shift in range(1, 5):
        upper = lax.slice_in_dim(padded, 4 + shift, 4 + shift + count, axis=axis)
        lower = lax.slice_in_dim(padded, 4 - shift, 4 - shift + count, axis=axis)
        lap = lap + COEFS[shift] * (upper + lower)
    return lap


def ham_slab(field, potential):
    padded_x = with_halo(field, (("grid", 1),), 4)
    lap = 3.0 * COEFS[0] * field
    lap = add_axis(lap, padded_x, 1, field.shape[1])
    lap = add_axis(lap, periodic_pad(field, 2), 2, field.shape[2])
    lap = add_axis(lap, periodic_pad(field, 3), 3, field.shape[3])
    return -0.5 * lap + potential[None] * field


def chebyshev(field, potential, operator):
    prev = field
    cur = (operator(field, potential) - CENTER * field) / HALF
    nxt = 2.0 * (operator(cur, potential) - CENTER * cur) / HALF - prev
    prev, cur = (cur, nxt)
    return cur


def lower_inverse(margin):
    factor = jnp.linalg.cholesky(margin)
    ident = jnp.eye(margin.shape[0], dtype=jnp.float32)
    return lax.linalg.triangular_solve(factor, ident, left_side=True, lower=True)


def body(orbitals, potential):
    cur = chebyshev(orbitals, potential, ham_slab)
    orb_count, planes, rows_y, rows_z = cur.shape
    groups = lax.axis_size("band")
    ncells = planes * lax.axis_size("grid") * rows_y * rows_z
    gathered = lax.all_gather(cur, "band", axis=0, tiled=True)
    own = cur.reshape(orb_count, -1)
    whole = gathered.reshape(orb_count * groups, -1)
    partial_value = jnp.dot(
        own, whole.T, precision=lax.Precision.HIGHEST, preferred_element_type=jnp.float32
    )
    rows = lax.psum(partial_value, "grid") / float(ncells)
    margin = lax.all_gather(rows, "band", axis=0, tiled=True)
    inverse = lower_inverse(margin)
    mine = lax.dynamic_slice_in_dim(inverse, lax.axis_index("band") * orb_count, orb_count, 0)
    result = jnp.dot(
        mine, whole, precision=lax.Precision.HIGHEST, preferred_element_type=jnp.float32
    )
    return result.reshape(orb_count, planes, rows_y, rows_z)


def solution(mesh):
    return jax.shard_map(
        body,
        mesh=mesh,
        in_specs=(P("band", "grid", None, None), P("grid", None, None)),
        out_specs=P("band", "grid", None, None),
        check_vma=False,
    )
```

profile of v0, /device:TPU:1, one launch (start us, length us, event | category | flops | bytes accessed | tf_op | source)
XLA Modules:
  0.0 881.5 jit_solution(5420446859480414676)
XLA Ops:
  6.5 1.8 copy.42
  8.4 3.7 collective-permute-start.1
  12.0 7.8 collective-permute-start
  20.0 0.4 fusion.121
  20.3 36.0 %collective-permute-done.1 = f32[64,4,8,128]{3,0,2,1:T(8,128)S(1)} collective-permute-done((f32[64,4,8,128]{3,0,2,1:T(8,128)S(1)}, f32[64,4,8,128]{3,0,2,1:T(8,128)S(1)}, u32[]{:S(2)}, u32[]{:S(2)}) %collective-permute-start.1) | collective-permute-done | bytes 1048608 | tf_op jit(solution)/shard_map/ppermute | solution.py:17
  56.5 0.6 constant_dynamic-update-slice_fusion.1
  57.1 1.2 collective-permute-done
  58.4 4.5 broadcast_multiply_fusion
  62.9 7.7 collective-permute-start.2
  70.7 0.4 fusion.118
  71.1 21.6 %collective-permute-done.2 = f32[64,4,8,128]{3,0,2,1:T(8,128)S(1)} collective-permute-done((f32[64,4,8,128]{3,0,2,1:T(8,128)S(1)}, f32[64,4,8,128]{3,0,2,1:T(8,128)S(1)}, u32[]{:S(2)}, u32[]{:S(2)}) %collective-permute-start.2) | collective-permute-done | bytes 1048608 | tf_op jit(solution)/shard_map/ppermute | solution.py:20
  92.7 19.7 %collective-permute-done.3 = f32[64,4,8,128]{3,0,2,1:T(8,128)S(1)} collective-permute-done((f32[64,4,8,128]{3,0,2,1:T(8,128)S(1)}, f32[64,4,8,128]{3,0,2,1:T(8,128)S(1)}, u32[]{:S(2)}, u32[]{:S(2)}) %collective-permute-start.3) | collective-permute-done | bytes 1048608 | tf_op jit(solution)/shard_map/ppermute | solution.py:17
  112.4 5.2 fusion.15
  117.7 52.1 %all-gather.2.cloned.1.call-done = f32[256,4,8,128]{3,0,2,1:T(8,128)} async-done(((f32[64,4,8,128]{3,0,2,1:T(8,128)}), f32[256,4,8,128]{3,0,2,1:T(8,128)}) %all-gather.2.cloned.1.call-update) | async-done | bytes 4194320 | tf_op jit(solution)/shard_map/all_gather | solution.py:68
  169.8 7.1 convolution_bitcast_fusion
  176.9 5.3 copy.59
  182.3 581.9 %all-reduce.3.cloned.1.call-done = f32[64,256]{1,0:T(8,128)} async-done(((f32[64,256]{1,0:T(8,128)}), f32[64,256]{1,0:T(8,128)}) %all-reduce.3.cloned.1.call-update) | async-done | bytes 65552 | tf_op jit(solution)/shard_map/psum | solution.py:74
  764.2 0.8 broadcast_multiply_fusion.1
  765.0 41.7 %all_gather.7 = f32[256,256]{1,0:T(8,128)S(1)} all-gather(f32[64,256]{1,0:T(8,128)S(1)} %broadcast_multiply_fusion.1), channel_id=1, replica_groups=mesh['band'=4,'grid'=64] {'band'}, dimensions={0}, use_global_device_ids=true | all-gather | bytes 327680 | tf_op jit(solution)/shard_map/all_gather | solution.py:75
  806.9 11.7 %cholesky.50 = f32[128,128]{1,0:T(8,128)S(1)} custom-call(f32[128,128]{1,0:T(8,128)S(1)} %cholesky.118), custom_call_target="Cholesky" | custom-call | tf_op jit(solution)/shard_map/jit(cholesky)/cholesky | solution.py:58
  818.7 9.8 %custom-call.14 = f32[1,128,128]{1,2,0:T(8,128)S(1)} custom-call(f32[1,128,128]{2,1,0:T(8,128)S(1)} %get-tuple-element.38), custom_call_target="InvertDiagBlocksLowerTriangular" | custom-call | tf_op jit(solution)/shard_map/jit(cholesky)/cholesky | solution.py:58
  829.0 11.7 %cholesky.105 = f32[128,128]{1,0:T(8,128)S(1)} custom-call(f32[128,128]{1,0:T(8,128)S(1)} %convolution_subtract_fusion.1), custom_call_target="Cholesky" | custom-call | tf_op jit(solution)/shard_map/jit(cholesky)/cholesky | solution.py:58
  840.8 0.6 compare_reduce_fusion
  842.7 4.0 while.1
  842.9 0.6 fusion.129
  843.5 1.3 bitcast_dynamic-update-slice_fusion.2
  844.8 0.6 fusion.129
  845.4 1.3 bitcast_dynamic-update-slice_fusion.2
  846.7 19.7 %custom-call.15 = f32[2,128,128]{1,2,0:T(8,128)S(1)} custom-call(f32[2,128,128]{2,1,0:T(8,128)S(1)} %get-tuple-element.12), custom_call_target="InvertDiagBlocksLowerTriangular" | custom-call | tf_op jit(solution)/shard_map/triangular_solve | solution.py:60
  867.0 0.3 fusion.110
  867.3 5.8 fusion
  873.1 1.6 copy.60
  (31 shorter events, 1.9 us)
Async XLA Ops:
  6.5 163.3 %all-gather.2.cloned.1.call-start = ((), (), s32[]{:S(2)}) async-start(), calls=%async_computation | async-start | bytes 5242880 | tf_op jit(solution)/shard_map/all_gather | solution.py:68
  8.4 47.9 %collective-permute-start.1 = (f32[64,4,8,128]{3,0,2,1:T(8,128)S(1)}, f32[64,4,8,128]{3,0,2,1:T(8,128)S(1)}, u32[]{:S(2)}, u32[]{:S(2)}) collective-permute-start(f32[64,4,8,128]{3,0,2,1:T(8,128)S(1)} %copy.42), channel_id=1, source_target_pairs={{0,1},{1,2},{2,3},{3,4},{4,5},{5,6},{6,7},{7,8},{8,9},{9,10},{10,1... | collective-permute-start | bytes 3145736 | tf_op jit(solution)/shard_map/ppermute | solution.py:17
  12.0 46.3 %collective-permute-start = (f32[64,4,8,128]{3,0,2,1:T(8,128)S(1)}, f32[64,4,8,128]{3,0,2,1:T(8,128)S(1)}, u32[]{:S(2)}, u32[]{:S(2)}) collective-permute-start(f32[64,4,8,128]{3,0,2,1:T(8,128)S(1)} %copy.42), channel_id=1, source_target_pairs={{1,0},{2,1},{3,2},{4,3},{5,4},{6,5},{7,6},{8,7},{9,8},{10,9},{11,1... | collective-permute-start | bytes 3145736 | tf_op jit(solution)/shard_map/ppermute | solution.py:20
  20.0 36.5 %copy-start = (f32[64,4,8,128]{3,2,1,0:T(8,128)S(1)}, f32[64,4,8,128]{3,2,1,0:T(8,128)}, u32[]{:S(2)}) copy-start(f32[64,4,8,128]{3,2,1,0:T(8,128)} %param.2) | copy-start | bytes 3145732
  56.4 2.0 copy-start.1
  62.9 29.8 %collective-permute-start.2 = (f32[64,4,8,128]{3,0,2,1:T(8,128)S(1)}, f32[64,4,8,128]{3,0,2,1:T(8,128)S(1)}, u32[]{:S(2)}, u32[]{:S(2)}) collective-permute-start(f32[64,4,8,128]{3,0,2,1:T(8,128)S(1)} %get-tuple-element.21), channel_id=1, source_target_pairs={{1,0},{2,1},{3,2},{4,3},{5,4},{6,5},{7,6},{8,7},{9,8},{10,9},{11,1... | collective-permute-start | bytes 3145736 | tf_op jit(solution)/shard_map/ppermute | solution.py:20
  70.6 41.8 %collective-permute-start.3 = (f32[64,4,8,128]{3,0,2,1:T(8,128)S(1)}, f32[64,4,8,128]{3,0,2,1:T(8,128)S(1)}, u32[]{:S(2)}, u32[]{:S(2)}) collective-permute-start(f32[64,4,8,128]{3,0,2,1:T(8,128)S(1)} %get-tuple-element.21), channel_id=1, source_target_pairs={{0,1},{1,2},{2,3},{3,4},{4,5},{5,6},{6,7},{7,8},{8,9},{9,10},{10,1... | collective-permute-start | bytes 3145736 | tf_op jit(solution)/shard_map/ppermute | solution.py:17
  117.6 646.6 %all-reduce.3.cloned.1.call-start = ((), (), s32[]{:S(2)}) async-start(), calls=%async_computation.1 | async-start | bytes 131072 | tf_op jit(solution)/shard_map/psum | solution.py:74
Sparse Core Ops, SparseCore 0:
  117.7 52.0 all-gather.1
  177.0 587.1 all-reduce.2
where the time goes:
time: 882 us
  waiting for transfers between devices  713 us (81%)
  other arithmetic  64.3 us (7%)
  blocking collectives  41.7 us (5%)
  starting transfers between devices  19.2 us (2%)
  between operations  14.8 us (2%)
  local copies, waits for them, and re-layouts  14.5 us (2%)
  matrix products  14.2 us (2%)
    psum x1, waiting for transfers between devices, body(): rows = lax.psum(partial_value, 'grid') / float(ncells)  582 us
    ppermute x2, waiting for transfers between devices, with_halo(): lax.ppermute(lax.slice_in_dim(block, block.shape[dim] - width, None, axis...  55.7 us
    all_gather x1, waiting for transfers between devices, body(): gathered = lax.all_gather(cur, 'band', axis=0, tiled=True)  52.1 us
    all_gather x1, blocking collectives, body(): margin = lax.all_gather(rows, 'band', axis=0, tiled=True)  41.7 us
    another operation x6, other arithmetic, lower_inverse(): factor = jnp.linalg.cholesky(margin)  33.9 us
    ppermute x2, waiting for transfers between devices, with_halo(): lax.ppermute(lax.slice_in_dim(block, 0, width, axis=dim), axis, backward)  22.8 us
    another operation x3, other arithmetic, lower_inverse(): lax.linalg.triangular_solve(factor, ident, left_side=True, lower=True)  19.7 us
  transfers between devices with their start and end apart: 6, of which 6 were waited for; matrix products, arithmetic and copies ran while one was open for 1% of the time, Pallas kernels for 0%

commit v1 on v0

--- a/solution.py
+++ b/solution.py
@@ -71,7 +71,7 @@
     partial_value = jnp.dot(
         own, whole.T, precision=lax.Precision.HIGHEST, preferred_element_type=jnp.float32
     )
-    rows = lax.psum(partial_value, "grid") / float(ncells)
+    rows = jnp.sum(lax.all_gather(partial_value, "grid"), axis=0) / float(ncells)
     margin = lax.all_gather(rows, "band", axis=0, tiled=True)
     inverse = lower_inverse(margin)
     mine = lax.dynamic_slice_in_dim(inverse, lax.axis_index("band") * orb_count, orb_count, 0)

time: 882 us -> 390 us (0.44)
  waiting for transfers between devices: 713 us -> 251 us
  blocking collectives: 41.7 us -> 10.1 us
    psum x1 -> x0, waiting for transfers between devices: 582 us -> none  [body(): rows = lax.psum(partial_value, 'grid') / float(ncells)]
    all_gather x0 -> x1, waiting for transfers between devices: none -> 120 us  [body(): lax.all_gather(partial_value, 'grid')]
    all_gather x1, blocking collectives: 41.7 us -> 10.1 us  [body(): margin = lax.all_gather(rows, 'band', axis=0, tiled=True)]
  transfers between devices with their start and end apart: 6 -> 6, of which waited for: 6 -> 6; matrix products, arithmetic and copies ran while one was open for 1% -> 2% of each run, Pallas kernels for 0% -> 0%
where the time goes in v1:
time: 390 us
  waiting for transfers between devices  251 us (64%)
  other arithmetic  65.9 us (17%)
  starting transfers between devices  19.2 us (5%)
  between operations  14.9 us (4%)
  local copies, waits for them, and re-layouts  14.6 us (4%)
  matrix products  14.2 us (4%)
  blocking collectives  10.1 us (3%)
    all_gather x1, waiting for transfers between devices, body(): lax.all_gather(partial_value, 'grid')  120 us
    ppermute x2, waiting for transfers between devices, with_halo(): lax.ppermute(lax.slice_in_dim(block, block.shape[dim] - width, None, axis...  55.7 us
    all_gather x1, waiting for transfers between devices, body(): gathered = lax.all_gather(cur, 'band', axis=0, tiled=True)  52.2 us
    another operation x6, other arithmetic, lower_inverse(): factor = jnp.linalg.cholesky(margin)  34 us
    ppermute x2, waiting for transfers between devices, with_halo(): lax.ppermute(lax.slice_in_dim(block, 0, width, axis=dim), axis, backward)  22.8 us
    another operation x3, other arithmetic, lower_inverse(): lax.linalg.triangular_solve(factor, ident, left_side=True, lower=True)  19.7 us
    ppermute x2, starting transfers between devices, with_halo(): lax.ppermute(lax.slice_in_dim(block, 0, width, axis=dim), axis, backward)  15.5 us
    all_gather x1, blocking collectives, body(): margin = lax.all_gather(rows, 'band', axis=0, tiled=True)  10.1 us
  transfers between devices with their start and end apart: 6, of which 6 were waited for; matrix products, arithmetic and copies ran while one was open for 2% of the time, Pallas kernels for 0%

profile of v1, /device:TPU:1, one launch (start us, length us, event | category | flops | bytes accessed | tf_op | source)
XLA Modules:
  0.0 389.7 jit_solution(10424450386847759747)
XLA Ops:
  6.5 1.8 copy.40
  8.4 3.7 collective-permute-start.1
  12.0 7.8 %collective-permute-start = (f32[64,4,8,128]{3,0,2,1:T(8,128)S(1)}, f32[64,4,8,128]{3,0,2,1:T(8,128)S(1)}, u32[]{:S(2)}, u32[]{:S(2)}) collective-permute-start(f32[64,4,8,128]{3,0,2,1:T(8,128)S(1)} %copy.40), channel_id=1, source_target_pairs={{1,0},{2,1},{3,2},{4,3},{5,4},{6,5},{7,6},{8,7},{9,8},{10,9},{11,1... | collective-permute-start | bytes 3145736 | tf_op jit(solution)/shard_map/ppermute | solution.py:20
  20.0 0.4 fusion.121
  20.3 36.0 %collective-permute-done.1 = f32[64,4,8,128]{3,0,2,1:T(8,128)S(1)} collective-permute-done((f32[64,4,8,128]{3,0,2,1:T(8,128)S(1)}, f32[64,4,8,128]{3,0,2,1:T(8,128)S(1)}, u32[]{:S(2)}, u32[]{:S(2)}) %collective-permute-start.1) | collective-permute-done | bytes 1048608 | tf_op jit(solution)/shard_map/ppermute | solution.py:17
  56.5 0.6 constant_dynamic-update-slice_fusion.1
  57.1 1.2 collective-permute-done
  58.4 4.5 %broadcast_multiply_fusion = (f32[64,4,8,128]{3,0,2,1:T(8,128)S(1)}, f32[64,4,8,128]{3,0,2,1:T(8,128)S(1)}) fusion(f32[64,4,8,128]{3,0,2,1:T(8,128)S(1)} %copy.40, f32[4,8,128]{2,1,0:T(8,128)S(1)} %copy-done.1, f32[64,4,8,4]{3,0,2,1:T(8,128)S(1)} %get-tuple-element.34, f32[64,4,8,4]{3,0,2,1:T(8,128)S(1)} %get-tuple-element.33, ...), kind=kLoop, calls=%fused_computation.177 | loop fusion | flops 15466496 | bytes 12664832 | tf_op jit(solution)/shard_map/div | solution.py:51
  62.9 7.7 %collective-permute-start.2 = (f32[64,4,8,128]{3,0,2,1:T(8,128)S(1)}, f32[64,4,8,128]{3,0,2,1:T(8,128)S(1)}, u32[]{:S(2)}, u32[]{:S(2)}) collective-permute-start(f32[64,4,8,128]{3,0,2,1:T(8,128)S(1)} %get-tuple-element.21), channel_id=1, source_target_pairs={{1,0},{2,1},{3,2},{4,3},{5,4},{6,5},{7,6},{8,7},{9,8},{10,9},{11,1... | collective-permute-start | bytes 3145736 | tf_op jit(solution)/shard_map/ppermute | solution.py:20
  70.7 0.4 fusion.118
  71.1 21.6 %collective-permute-done.2 = f32[64,4,8,128]{3,0,2,1:T(8,128)S(1)} collective-permute-done((f32[64,4,8,128]{3,0,2,1:T(8,128)S(1)}, f32[64,4,8,128]{3,0,2,1:T(8,128)S(1)}, u32[]{:S(2)}, u32[]{:S(2)}) %collective-permute-start.2) | collective-permute-done | bytes 1048608 | tf_op jit(solution)/shard_map/ppermute | solution.py:20
  92.7 19.7 %collective-permute-done.3 = f32[64,4,8,128]{3,0,2,1:T(8,128)S(1)} collective-permute-done((f32[64,4,8,128]{3,0,2,1:T(8,128)S(1)}, f32[64,4,8,128]{3,0,2,1:T(8,128)S(1)}, u32[]{:S(2)}, u32[]{:S(2)}) %collective-permute-start.3) | collective-permute-done | bytes 1048608 | tf_op jit(solution)/shard_map/ppermute | solution.py:17
  112.4 5.2 %fusion.15 = f32[64,4,8,128]{3,0,2,1:T(8,128)} fusion(f32[64,4,8,128]{3,0,2,1:T(8,128)S(1)} %get-tuple-element.21, f32[64,4,4,128]{3,0,2,1:T(8,128)S(1)} %get-tuple-element.28, f32[64,4,4,128]{3,0,2,1:T(8,128)S(1)} %get-tuple-element.27, f32[64,4,8,128]{3,0,2,1:T(8,128)S(1)} %collective-permute-done.3, f32[64,4,8,128]{3,0,2,1:T(8,128)S(1)} %collective-permute-done.2, ...), kind=kLoop, calls=%fused_computation.76 | loop fusion | flops 17301504 | bytes 7421952 | tf_op jit(solution)/shard_map/sub | solution.py:52
  117.6 52.2 %all-gather.4.cloned.1.call-done = f32[256,4,8,128]{3,0,2,1:T(8,128)} async-done(((f32[64,4,8,128]{3,0,2,1:T(8,128)}), f32[256,4,8,128]{3,0,2,1:T(8,128)}) %all-gather.4.cloned.1.call-update) | async-done | bytes 4194320 | tf_op jit(solution)/shard_map/all_gather | solution.py:68
  169.8 7.1 %convolution_bitcast_fusion = f32[64,256]{1,0:T(8,128)} fusion(f32[64,4,8,128]{3,0,2,1:T(8,128)} %fusion.15, f32[256,4,8,128]{3,0,2,1:T(8,128)} %all-gather.4.cloned.1.call-done), kind=kOutput, calls=%fused_computation.62 | convolution fusion | flops 805306368 | bytes 5308416 | tf_op jit(solution)/shard_map/dot_general | solution.py:71
  177.0 5.3 %copy.57 = f32[256,4,8,128]{0,3,2,1:T(8,128)} copy(f32[256,4,8,128]{3,0,2,1:T(8,128)} %all-gather.4.cloned.1.call-done) | data formatting | bytes 8388608 | tf_op jit(solution)/shard_map/all_gather | solution.py:68
  182.3 119.9 %all-gather.6.cloned.1.call-done = f32[4096,256]{1,0:T(8,128)} async-done(((f32[64,256]{1,0:T(8,128)}), f32[4096,256]{1,0:T(8,128)}) %all-gather.6.cloned.1.call-update) | async-done | bytes 4194320 | tf_op jit(solution)/shard_map/all_gather | solution.py:74
  302.2 2.4 reduce_sum.9
  304.7 10.1 %all_gather.15 = f32[256,256]{1,0:T(8,128)S(1)} all-gather(f32[64,256]{1,0:T(8,128)S(1)} %broadcast_multiply_fusion.1), channel_id=1, replica_groups=mesh['band'=4,'grid'=64] {'band'}, dimensions={0}, use_global_device_ids=true | all-gather | bytes 327680 | tf_op jit(solution)/shard_map/all_gather | solution.py:75
  314.9 11.7 %cholesky.50 = f32[128,128]{1,0:T(8,128)S(1)} custom-call(f32[128,128]{1,0:T(8,128)S(1)} %cholesky.118), custom_call_target="Cholesky" | custom-call | tf_op jit(solution)/shard_map/jit(cholesky)/cholesky | solution.py:58
  326.7 9.8 %custom-call.14 = f32[1,128,128]{1,2,0:T(8,128)S(1)} custom-call(f32[1,128,128]{2,1,0:T(8,128)S(1)} %get-tuple-element.38), custom_call_target="InvertDiagBlocksLowerTriangular" | custom-call | tf_op jit(solution)/shard_map/jit(cholesky)/cholesky | solution.py:58
  337.0 11.7 %cholesky.105 = f32[128,128]{1,0:T(8,128)S(1)} custom-call(f32[128,128]{1,0:T(8,128)S(1)} %convolution_subtract_fusion.1), custom_call_target="Cholesky" | custom-call | tf_op jit(solution)/shard_map/jit(cholesky)/cholesky | solution.py:58
  348.8 0.7 compare_reduce_fusion
  350.8 4.0 %while.1 = (s32[]{:T(128)}, f32[256,256]{1,0:T(8,128)S(1)}, s32[2,2]{1,0:T(2,128)S(1)}, f32[2,128,128]{2,1,0:T(8,128)S(1)}, s32[]{:T(128)}) while((s32[]{:T(128)}, f32[256,256]{1,0:T(8,128)S(1)}, s32[2,2]{1,0:T(2,128)S(1)}, f32[2,128,128]{2,1,0:T(8,128)S(1)}, s32[]{:T(128)}) %tuple.29), condition=%wide.while_cond, body=%wide.while_body.sunk | while | flops 2 | bytes 131181 | solution.py:60
  351.0 0.6 fusion.129
  351.6 1.3 bitcast_dynamic-update-slice_fusion.2
  352.9 0.6 fusion.129
  353.5 1.3 bitcast_dynamic-update-slice_fusion.2
  354.9 19.7 %custom-call.15 = f32[2,128,128]{1,2,0:T(8,128)S(1)} custom-call(f32[2,128,128]{2,1,0:T(8,128)S(1)} %get-tuple-element.12), custom_call_target="InvertDiagBlocksLowerTriangular" | custom-call | tf_op jit(solution)/shard_map/triangular_solve | solution.py:60
  375.1 0.3 fusion.110
  375.4 5.8 %fusion = f32[64,4,8,128]{3,0,2,1:T(8,128)S(1)} fusion(f32[256,4,8,128]{0,3,2,1:T(8,128)} %copy.57, s32[]{:T(128)S(6)} %select_n.8, f32[128,256]{1,0:T(8,128)S(1)} %fusion.104, f32[128,256]{1,0:T(8,128)S(1)} %fusion.110), kind=kOutput, calls=%fused_computation.2 | convolution fusion | flops 805322752 | bytes 5505028 | tf_op jit(solution)/shard_map/dot_general | solution.py:78
  381.3 1.6 copy.58
  (32 shorter events, 1.9 us)
Async XLA Ops:
  6.5 163.3 %all-gather.4.cloned.1.call-start = ((), (), s32[]{:S(2)}) async-start(), calls=%async_computation | async-start | bytes 5242880 | tf_op jit(solution)/shard_map/all_gather | solution.py:68
  8.4 47.9 %collective-permute-start.1 = (f32[64,4,8,128]{3,0,2,1:T(8,128)S(1)}, f32[64,4,8,128]{3,0,2,1:T(8,128)S(1)}, u32[]{:S(2)}, u32[]{:S(2)}) collective-permute-start(f32[64,4,8,128]{3,0,2,1:T(8,128)S(1)} %copy.40), channel_id=1, source_target_pairs={{0,1},{1,2},{2,3},{3,4},{4,5},{5,6},{6,7},{7,8},{8,9},{9,10},{10,1... | collective-permute-start | bytes 3145736 | tf_op jit(solution)/shard_map/ppermute | solution.py:17
  12.0 46.3 %collective-permute-start = (f32[64,4,8,128]{3,0,2,1:T(8,128)S(1)}, f32[64,4,8,128]{3,0,2,1:T(8,128)S(1)}, u32[]{:S(2)}, u32[]{:S(2)}) collective-permute-start(f32[64,4,8,128]{3,0,2,1:T(8,128)S(1)} %copy.40), channel_id=1, source_target_pairs={{1,0},{2,1},{3,2},{4,3},{5,4},{6,5},{7,6},{8,7},{9,8},{10,9},{11,1... | collective-permute-start | bytes 3145736 | tf_op jit(solution)/shard_map/ppermute | solution.py:20
  20.0 36.5 %copy-start = (f32[64,4,8,128]{3,2,1,0:T(8,128)S(1)}, f32[64,4,8,128]{3,2,1,0:T(8,128)}, u32[]{:S(2)}) copy-start(f32[64,4,8,128]{3,2,1,0:T(8,128)} %param.2) | copy-start | bytes 3145732
  56.4 2.0 copy-start.1
  62.9 29.8 %collective-permute-start.2 = (f32[64,4,8,128]{3,0,2,1:T(8,128)S(1)}, f32[64,4,8,128]{3,0,2,1:T(8,128)S(1)}, u32[]{:S(2)}, u32[]{:S(2)}) collective-permute-start(f32[64,4,8,128]{3,0,2,1:T(8,128)S(1)} %get-tuple-element.21), channel_id=1, source_target_pairs={{1,0},{2,1},{3,2},{4,3},{5,4},{6,5},{7,6},{8,7},{9,8},{10,9},{11,1... | collective-permute-start | bytes 3145736 | tf_op jit(solution)/shard_map/ppermute | solution.py:20
  70.6 41.8 %collective-permute-start.3 = (f32[64,4,8,128]{3,0,2,1:T(8,128)S(1)}, f32[64,4,8,128]{3,0,2,1:T(8,128)S(1)}, u32[]{:S(2)}, u32[]{:S(2)}) collective-permute-start(f32[64,4,8,128]{3,0,2,1:T(8,128)S(1)} %get-tuple-element.21), channel_id=1, source_target_pairs={{0,1},{1,2},{2,3},{3,4},{4,5},{5,6},{6,7},{7,8},{8,9},{9,10},{10,1... | collective-permute-start | bytes 3145736 | tf_op jit(solution)/shard_map/ppermute | solution.py:17
  117.6 184.6 %all-gather.6.cloned.1.call-start = ((), (), s32[]{:S(2)}) async-start(), calls=%async_computation.1 | async-start | bytes 4259840 | tf_op jit(solution)/shard_map/all_gather | solution.py:74
Sparse Core Ops, SparseCore 0:
  117.7 52.0 all-gather.3
  177.0 125.1 all-gather.5
